TPU v7x, 32 devices: a whole 2x2x4 slice. The times are simulated.
32 devices in a mesh: dp: 4 (over y, x), seq: 4 (over z), expert: 2 (over core).
Axes of the slice: x: 2, y: 2, z: 4, core: 2. Of those that a mesh axis runs over, the one named last changes fastest.
Arguments:
- queries: bfloat16 [8, 512, 2048], P(('dp', 'expert'), 'seq'), may hold values from -135 to 135
- keys: bfloat16 [8, 512, 2048], P(('dp', 'expert'), 'seq'), may hold values from -5 to 5
- values: bfloat16 [8, 512, 2048], P(('dp', 'expert'), 'seq'), may hold values from -6 to 6
- resid: bfloat16 [8, 512, 2048], P(('dp', 'expert'), 'seq'), may hold values from -20 to 20
- cotangent: bfloat16 [8, 512, 2048], P(('dp', 'expert'), 'seq'), may hold values from -0.3125 to 0.3125
- zone_ids: int32 [8, 512, 1], P(('dp', 'expert'), 'seq'), may hold values from 0 to 7; in each aligned block of 128 rows (0 to 127, 128 to 255, ..., all dimensions but the last counted through in order) at most 34 rows name the same one
- norm_gain: float32 [2048], replicated, may hold values from 0.1 to 1.9
- w_in: bfloat16 [8, 2048, 4096], P(('seq', 'expert'), None, 'dp'), may hold values from -0.125 to 0.125
- w_out: bfloat16 [8, 4096, 2048], P(('seq', 'expert'), 'dp'), may hold values from -0.09375 to 0.09375
Outputs:
- layer_out: bfloat16 [8, 512, 2048], P(('dp', 'expert'), 'seq')
- grad_w_in: bfloat16 [8, 2048, 4096], P(('seq', 'expert'), None, 'dp')
- grad_w_out: bfloat16 [8, 4096, 2048], P(('seq', 'expert'), 'dp')
Inputs may be any that keep to these rules, and one draw needn't show every extreme that they name: `zone_ids`: among the tokens of one device at most 34 name the same expert, and that count is reached.
All inputs are finite; a program needn't handle non-finite values.
Results may differ from a plain program's by a relative error of at most 0.0085.
Values may be sent and summed in bfloat16 or wider, within the bound.
A program may use at most 128 MiB of HBM per device.

v0:
```python
import math
import jax
import jax.numpy as jnp
from jax import lax
from jax.sharding import PartitionSpec as P

HEADS = 16
epsilon = 1e-05


def shards(queries, keys, values, resid, cotangent, zone_ids, norm_gain, w_in, w_out):
    local_rows = queries.shape[1]
    model_width = queries.shape[2]
    head_dim = model_width // HEADS
    score_scale = 1.0 / math.sqrt(head_dim)
    q_heads = queries[0].reshape(local_rows, HEADS, head_dim)
    peak_now = jnp.full((HEADS, local_rows), -jnp.inf, jnp.float32)
    totals = jnp.zeros((HEADS, local_rows), jnp.float32)
    accum = jnp.zeros((HEADS, local_rows, head_dim), jnp.float32)
    key_block = lax.all_gather(keys, "seq", axis=1, tiled=True)
    value_block = lax.all_gather(values, "seq", axis=1, tiled=True)
    count = key_block.shape[1]
    k_heads = key_block[0].reshape(count, HEADS, head_dim)
    v_heads = value_block[0].reshape(count, HEADS, head_dim)
    scores = (
        jnp.einsum("shd,thd->hst", q_heads, k_heads, preferred_element_type=jnp.float32)
        * score_scale
    )
    newest = jnp.max(scores, axis=-1)
    factor = jnp.exp(peak_now - newest)
    weights = jnp.exp(scores - newest[..., None])
    totals = totals * factor + jnp.sum(weights, axis=-1)
    accum = accum * factor[..., None] + jnp.einsum(
        "hst,thd->hsd", weights.astype(jnp.bfloat16), v_heads, preferred_element_type=jnp.float32
    )
    peak_now, totals, accum = (newest, totals, accum)
    attended = (accum / totals[..., None]).transpose(1, 0, 2).reshape(local_rows, model_width)
    mixed = resid[0].astype(jnp.float32) + attended
    mean_sq = jnp.mean(mixed * mixed, axis=-1, keepdims=True)
    normed = (mixed * lax.rsqrt(mean_sq + epsilon) * norm_gain).astype(jnp.bfloat16)
    owners = lax.axis_size("seq") * lax.axis_size("expert")
    groups = lax.axis_size("dp")
    capacity = 2 * local_rows // owners + 2
    zone_of = zone_ids[0, :, 0]
    expert_hot = (zone_of[:, None] == jnp.arange(owners, dtype=jnp.int32)[None, :]).astype(
        jnp.int32
    )
    ranking = jnp.cumsum(expert_hot, axis=0) - 1
    slot_index = jnp.sum(ranking * expert_hot, axis=1)
    target = zone_of * capacity + slot_index
    placing = (target[None, :] == jnp.arange(owners * capacity, dtype=jnp.int32)[:, None]).astype(
        jnp.bfloat16
    )
    send_x = jnp.dot(placing, normed, preferred_element_type=jnp.float32).astype(jnp.bfloat16)
    send_g = jnp.dot(placing, cotangent[0], preferred_element_type=jnp.float32).astype(jnp.bfloat16)
    send_x = send_x.reshape(owners, capacity, model_width)
    send_g = send_g.reshape(owners, capacity, model_width)
    row_x, row_g = (
        lax.all_to_all(send_x, ("seq", "expert"), split_axis=0, concat_axis=0, tiled=True),
        lax.all_to_all(send_g, ("seq", "expert"), split_axis=0, concat_axis=0, tiled=True),
    )
    arrived_x, arrived_g = (
        lax.all_gather(row_x, "dp", axis=0, tiled=True),
        lax.all_gather(row_g, "dp", axis=0, tiled=True),
    )
    slot_count = groups * owners * capacity
    inputs = arrived_x.reshape(slot_count, model_width)
    grads_in = arrived_g.reshape(slot_count, model_width)
    w_first = w_in[0]
    w_second = w_out[0]
    pre_act = jnp.dot(inputs, w_first, preferred_element_type=jnp.float32)
    activated, pull_back = jax.vjp(jax.nn.gelu, pre_act)
    hidden = activated.astype(jnp.bfloat16)
    back_proj = lax.dot_general(
        grads_in, w_second, (((1,), (1,)), ((), ())), preferred_element_type=jnp.float32
    )
    d_pre = pull_back(back_proj)[0].astype(jnp.bfloat16)
    grad_first = lax.dot_general(
        inputs, d_pre, (((0,), (0,)), ((), ())), preferred_element_type=jnp.float32
    ).astype(jnp.bfloat16)
    grad_second = lax.dot_general(
        hidden, grads_in, (((0,), (0,)), ((), ())), preferred_element_type=jnp.float32
    ).astype(jnp.bfloat16)
    summed = lax.psum_scatter(
        jnp.dot(hidden, w_second, preferred_element_type=jnp.float32).astype(jnp.bfloat16),
        "dp",
        scatter_dimension=0,
        tiled=True,
    )
    returned = lax.all_to_all(
        summed.reshape(owners, capacity, model_width),
        ("seq", "expert"),
        split_axis=0,
        concat_axis=0,
        tiled=True,
    )
    expert_rows = lax.dot_general(
        placing,
        returned.reshape(owners * capacity, model_width),
        (((0,), (0,)), ((), ())),
        preferred_element_type=jnp.float32,
    )
    layer_out = (mixed + expert_rows).astype(jnp.bfloat16)[None]
    return (layer_out, grad_first[None], grad_second[None])


def solution(mesh):
    placed = (
        P(("dp", "expert"), "seq", None),
        P(("dp", "expert"), "seq", None),
        P(("dp", "expert"), "seq", None),
        P(("dp", "expert"), "seq", None),
        P(("dp", "expert"), "seq", None),
        P(("dp", "expert"), "seq", None),
        P(),
        P(("seq", "expert"), None, "dp"),
        P(("seq", "expert"), "dp", None),
    )
    return jax.shard_map(
        shards,
        mesh=mesh,
        in_specs=placed,
        out_specs=(
            P(("dp", "expert"), "seq", None),
            P(("seq", "expert"), None, "dp"),
            P(("seq", "expert"), "dp", None),
        ),
        check_vma=False,
    )
```

profile of v0, /device:TPU:0, one launch (start us, length us, event | category | flops | bytes accessed | tf_op | source)
XLA Modules:
  0.0 370.8 jit_solution(17556214826301399096)
XLA Ops:
  7.2 0.0 all-gather.5.cloned.1.call-start
  7.2 2.1 copy.22
  9.3 0.0 all-gather.5.cloned.1.call-update
  9.3 0.0 all-gather.7.cloned.1.call-start
  9.4 0.7 all-gather.7.cloned.1.call-update
  10.1 0.0 all-gather.9.cloned.1.call-start
  10.1 1.1 copy.33
  11.3 2.2 copy.27
  13.5 0.1 fusion.42
  13.6 0.2 reduce_window_sum.11
  13.8 0.2 select_reduce_fusion
  14.0 45.2 %all-gather.5.cloned.1.call-done = bf16[1,512,2048]{1,2,0:T(8,128)(2,1)} async-done(((bf16[1,128,2048]{1,2,0:T(8,128)(2,1)}), bf16[1,512,2048]{1,2,0:T(8,128)(2,1)}) %all-gather.5.cloned.1.call-update) | async-done | bytes 2097168 | tf_op jit(solution)/shard_map/all_gather | solution.py:20
  59.2 2.4 multiply_reduce_fusion
  61.6 2.0 copy-done.2
  63.6 1.3 fusion.14
  64.9 39.7 %all-gather.7.cloned.1.call-done = bf16[1,512,2048]{2,1,0:T(8,128)(2,1)} async-done(((bf16[1,128,2048]{2,1,0:T(8,128)(2,1)}), bf16[1,512,2048]{2,1,0:T(8,128)(2,1)}) %all-gather.7.cloned.1.call-update) | async-done | bytes 2097168 | tf_op jit(solution)/shard_map/all_gather | solution.py:21
  104.6 2.9 copy.25
  107.5 4.7 %multiply_reduce_fusion.1 = (f32[128]{0:T(128)S(1)}, f32[128,16,128]{0,2,1:T(8,128)}) fusion(f32[128,16,128]{0,2,1:T(8,128)} %bitcast.59, f32[128,16]{0,1:T(8,128)S(1)} %bitcast_add_fusion.2, bf16[512,16,128]{0,2,1:T(8,128)(2,1)S(1)} %bitcast.56, f32[16,128,512]{2,1,0:T(8,128)} %copy-done.2, f32[16,128]{1,0:T(8,128)S(1)} %get-tuple-element.3, ...), kind=kOutput, calls=%fused_computation.34 | convolution fusion | flops 272891776 | bytes 8413696 | tf_op jit(solution)/shard_map/hst,thd->hsd/dot_general | solution.py:33
  112.2 1.6 copy.26
  113.8 1.5 convolution_convert_fusion.2
  115.3 1.4 reshape.62
  116.7 34.6 %all_to_all.15 = bf16[8,34,2048]{2,1,0:T(8,128)(2,1)S(1)} all-to-all(bf16[8,34,2048]{2,1,0:T(8,128)(2,1)S(1)} %reshape.62), channel_id=1, replica_groups=mesh['dp'=4,'seq'=4,'expert'=2] {'seq','expert'}, dimensions={0} | all-to-all | bytes 2228224 | tf_op jit(solution)/shard_map/all_to_all | solution.py:59
  151.3 1.6 copy.28
  153.0 0.0 all-gather.11.cloned.1.call-start
  153.0 1.4 convolution_convert_fusion.1
  154.5 1.4 reshape.66
  155.9 34.6 %all_to_all.16 = bf16[8,34,2048]{2,1,0:T(8,128)(2,1)S(1)} all-to-all(bf16[8,34,2048]{2,1,0:T(8,128)(2,1)S(1)} %reshape.66), channel_id=1, replica_groups=mesh['dp'=4,'seq'=4,'expert'=2] {'seq','expert'}, dimensions={0} | all-to-all | bytes 2228224 | tf_op jit(solution)/shard_map/all_to_all | solution.py:60
  190.5 1.6 copy.30
  192.1 0.0 all-gather.11.cloned.1.call-update
  192.1 0.0 reduce-scatter.2.cloned.1.call-start
  192.2 14.5 %all-gather.9.cloned.1.call-done = bf16[32,34,2048]{2,0,1:T(8,128)(2,1)} async-done(((bf16[8,34,2048]{2,0,1:T(8,128)(2,1)}), bf16[32,34,2048]{2,0,1:T(8,128)(2,1)}) %all-gather.9.cloned.1.call-update) | async-done | bytes 4456464 | tf_op jit(solution)/shard_map/all_gather | solution.py:63
  206.7 7.1 %copy.29 = bf16[32,34,2048]{2,1,0:T(8,128)(2,1)} copy(bf16[32,34,2048]{2,0,1:T(8,128)(2,1)} %all-gather.9.cloned.1.call-done) | data formatting | bytes 8912896 | tf_op jit(solution)/shard_map/all_gather | solution.py:63
  213.8 7.5 %reshape.63 = bf16[1088,2048]{1,0:T(8,128)(2,1)} reshape(bf16[32,34,2048]{2,1,0:T(8,128)(2,1)} %copy.29) | data formatting | bytes 8912896 | tf_op jit(solution)/shard_map/reshape | solution.py:67
  221.3 8.0 %fusion.12 = f32[1088,1024]{1,0:T(8,128)S(1)} fusion(bf16[1088,2048]{1,0:T(8,128)(2,1)} %reshape.63, bf16[1,2048,1024]{2,1,0:T(8,128)(2,1)} %param.16), kind=kOutput, calls=%fused_computation.14 | convolution fusion | flops 4563402752 | bytes 13107200 | tf_op jit(solution)/shard_map/dot_general | solution.py:71
  229.2 2.1 copy-done.7
  231.4 6.9 %convolution_convert_fusion = bf16[1088,2048]{1,0:T(8,128)(2,1)} fusion(bf16[1,1024,2048]{2,1,0:T(8,128)(2,1)S(1)} %copy-done.6, f32[1088,1024]{1,0:T(8,128)S(1)} %fusion.12), kind=kOutput, calls=%fused_computation | convolution fusion | flops 4575657984 | bytes 13107200 | tf_op jit(solution)/shard_map/dot_general | solution.py:85
  238.3 0.0 reduce-scatter.2.cloned.1.call-update
  238.3 25.5 %all-gather.11.cloned.1.call-done = bf16[32,34,2048]{2,0,1:T(8,128)(2,1)} async-done(((bf16[8,34,2048]{2,0,1:T(8,128)(2,1)}), bf16[32,34,2048]{2,0,1:T(8,128)(2,1)}) %all-gather.11.cloned.1.call-update) | async-done | bytes 4456464 | tf_op jit(solution)/shard_map/all_gather | solution.py:64
  263.8 7.1 %copy.31 = bf16[32,34,2048]{2,1,0:T(8,128)(2,1)} copy(bf16[32,34,2048]{2,0,1:T(8,128)(2,1)} %all-gather.11.cloned.1.call-done) | data formatting | bytes 8912896 | tf_op jit(solution)/shard_map/all_gather | solution.py:64
  270.8 7.4 %reshape.67 = bf16[1088,2048]{1,0:T(8,128)(2,1)} reshape(bf16[32,34,2048]{2,1,0:T(8,128)(2,1)} %copy.31) | data formatting | bytes 8912896 | tf_op jit(solution)/shard_map/reshape | solution.py:68
  278.3 10.7 %convert_bitcast_fusion = bf16[1,1024,2048]{2,1,0:T(8,128)(2,1)} fusion(bf16[1088,2048]{1,0:T(8,128)(2,1)} %reshape.67, f32[1088,1024]{1,0:T(8,128)} %copy-done.7), kind=kOutput, calls=%fused_computation.16 | convolution fusion | flops 4575526912 | bytes 13107200 | tf_op jit(solution)/shard_map/dot_general | solution.py:81
  289.0 32.5 %reduce-scatter.2.cloned.1.call-done = bf16[272,2048]{1,0:T(8,128)(2,1)} async-done(((bf16[1088,2048]{1,0:T(8,128)(2,1)}), bf16[272,2048]{1,0:T(8,128)(2,1)}) %reduce-scatter.2.cloned.1.call-update) | async-done | bytes 1114128 | tf_op jit(solution)/shard_map/reduce_scatter | solution.py:84
  321.5 2.3 reshape.64
  323.8 4.6 %all-to-all-start.1 = ((bf16[8,34,2048]{2,1,0:T(8,128)(2,1)}), bf16[8,34,2048]{2,1,0:T(8,128)(2,1)S(1)}, u32[]{:S(2)}, u32[]{:S(2)}) async-start(bf16[8,34,2048]{2,1,0:T(8,128)(2,1)} %reshape.64), calls=%async_computation.2 | async-start | bytes 2621440 | tf_op jit(solution)/shard_map/all_to_all | solution.py:90
  328.4 18.7 %convert_bitcast_fusion.1 = bf16[1,2048,1024]{2,1,0:T(8,128)(2,1)} fusion(bf16[1088,2048]{1,0:T(8,128)(2,1)} %reshape.63, f32[1088,1024]{1,0:T(8,128)} %copy-done.7, bf16[1088,2048]{1,0:T(8,128)(2,1)} %reshape.67, bf16[1,1024,2048]{2,1,0:T(8,128)(2,1)} %param.17), kind=kOutput, calls=%fused_computation.17 | convolution fusion | flops 9151184896 | bytes 21757952 | tf_op jit(solution)/shard_map/dot_general | solution.py:78
  347.1 13.5 %all-to-all-done.1 = bf16[8,34,2048]{2,1,0:T(8,128)(2,1)S(1)} async-done(((bf16[8,34,2048]{2,1,0:T(8,128)(2,1)}), bf16[8,34,2048]{2,1,0:T(8,128)(2,1)S(1)}, u32[]{:S(2)}, u32[]{:S(2)}) %all-to-all-start.1) | async-done | bytes 1114144 | tf_op jit(solution)/shard_map/all_to_all | solution.py:90
  360.6 1.2 reshape.65
  361.7 2.5 fusion.17
  (19 shorter events, 0.1 us)
Async XLA Ops:
  7.2 145.9 %copy-start = (bf16[1,128,2048]{2,1,0:T(8,128)(2,1)S(1)}, bf16[1,128,2048]{2,1,0:T(8,128)(2,1)}, u32[]{:S(2)}) copy-start(bf16[1,128,2048]{2,1,0:T(8,128)(2,1)} %param.13) | copy-start | bytes 1572868
  7.2 6.3 %copy-start.5 = (s32[1,128,1]{1,2,0:T(1,128)S(1)}, s32[1,128,1]{1,2,0:T(1,128)}, u32[]{:S(2)}) copy-start(s32[1,128,1]{1,2,0:T(1,128)} %param.14) | copy-start | bytes 1540
  7.2 52.0 %all-gather.5.cloned.1.call-start = ((), (), s32[]{:S(2)}) async-start(), calls=%async_computation.4 | async-start | bytes 2621440 | tf_op jit(solution)/shard_map/all_gather | solution.py:20
  9.3 95.2 %all-gather.7.cloned.1.call-start = ((), (), s32[]{:S(2)}) async-start(), calls=%async_computation.5 | async-start | bytes 2621440 | tf_op jit(solution)/shard_map/all_gather | solution.py:21
  10.1 196.6 %all-gather.9.cloned.1.call-start = ((), (), s32[]{:S(2)}) async-start(), calls=%async_computation.6 | async-start | bytes 5570560 | tf_op jit(solution)/shard_map/all_gather | solution.py:63
  61.5 2.0 copy-start.2
  107.5 6.3 %copy-start.3 = (bf16[1,128,2048]{2,1,0:T(8,128)(2,1)S(1)}, bf16[1,128,2048]{2,1,0:T(8,128)(2,1)}, u32[]{:S(2)}) copy-start(bf16[1,128,2048]{2,1,0:T(8,128)(2,1)} %param.12) | copy-start | bytes 1572868
  107.5 6.3 %copy-start.4 = (f32[2048]{0:T(1024)S(1)}, f32[2048]{0:T(1024)}, u32[]{:S(2)}) copy-start(f32[2048]{0:T(1024)} %param.15) | copy-start | bytes 24580
  153.0 110.8 %all-gather.11.cloned.1.call-start = ((), (), s32[]{:S(2)}) async-start(), calls=%async_computation.8 | async-start | bytes 5570560 | tf_op jit(solution)/shard_map/all_gather | solution.py:64
  192.1 129.4 %reduce-scatter.2.cloned.1.call-start = ((), (), s32[]{:S(2)}) async-start(), calls=%async_computation.7 | async-start | bytes 5570560 | tf_op jit(solution)/shard_map/reduce_scatter | solution.py:84
  221.3 10.1 %copy-start.6 = (bf16[1,1024,2048]{2,1,0:T(8,128)(2,1)S(1)}, bf16[1,1024,2048]{2,1,0:T(8,128)(2,1)}, u32[]{:S(2)}) copy-start(bf16[1,1024,2048]{2,1,0:T(8,128)(2,1)} %param.17) | copy-start | bytes 12582916
  229.2 2.1 copy-start.7
  323.8 36.8 %all-to-all-start.1 = ((bf16[8,34,2048]{2,1,0:T(8,128)(2,1)}), bf16[8,34,2048]{2,1,0:T(8,128)(2,1)S(1)}, u32[]{:S(2)}, u32[]{:S(2)}) async-start(bf16[8,34,2048]{2,1,0:T(8,128)(2,1)} %reshape.64), calls=%async_computation.2 | async-start | bytes 2621440 | tf_op jit(solution)/shard_map/all_to_all | solution.py:90
  328.4 35.9 %copy-start.1 = (bf16[1,128,2048]{2,1,0:T(8,128)(2,1)S(1)}, bf16[1,128,2048]{2,1,0:T(8,128)(2,1)}, u32[]{:S(2)}) copy-start(bf16[1,128,2048]{2,1,0:T(8,128)(2,1)} %param.13) | copy-start | bytes 1572868
Sparse Core Ops, SparseCore 0:
  10.1 48.9 all-gather.4
  60.7 43.8 all-gather.6
  153.1 53.5 all-gather.8
  209.0 54.7 all-gather.10
  266.7 54.7 reduce-scatter.1
where the time goes:
time: 372 us; the launch traced here: 371 us
  waiting for transfers between devices  172 us (46%)
  blocking collectives  69.2 us (19%)
  matrix products  56.8 us (15%)
  local copies, waits for them, and re-layouts  52.5 us (14%)
  between operations  13.9 us (4%)
  starting transfers between devices  4.81 us (1%)
    all_gather x1, waiting for transfers between devices, shards(): key_block = lax.all_gather(keys, 'seq', axis=1, tiled=True)  45.2 us
    all_gather x1, waiting for transfers between devices, shards(): value_block = lax.all_gather(values, 'seq', axis=1, tiled=True)  39.7 us
    all_to_all x1, blocking collectives, shards(): lax.all_to_all(send_x, ('seq', 'expert'), split_axis=0, concat_axis=0, ti...  34.6 us
    all_to_all x1, blocking collectives, shards(): lax.all_to_all(send_g, ('seq', 'expert'), split_axis=0, concat_axis=0, ti...  34.6 us
    reduce_scatter x1, waiting for transfers between devices, shards(): lax.psum_scatter(jnp.dot(hidden, w_second, preferred_element_type=jnp.flo...  32.5 us
    all_gather x1, waiting for transfers between devices, shards(): lax.all_gather(row_g, 'dp', axis=0, tiled=True)  25.5 us
    dot_general x1, matrix products, shards(): lax.dot_general(inputs, d_pre, (((0,), (0,)), ((), ())), preferred_elemen...  18.7 us
    all_gather x1, waiting for transfers between devices, shards(): lax.all_gather(row_x, 'dp', axis=0, tiled=True)  14.5 us
  transfers between devices with their start and end apart: 6, of which 6 were waited for; matrix products, arithmetic and copies ran while one was open for 23% of the time, Pallas kernels for 0%

commit v1 on v0

--- a/solution.py
+++ b/solution.py
@@ -9,6 +9,26 @@
 
 
 def shards(queries, keys, values, resid, cotangent, zone_ids, norm_gain, w_in, w_out):
+
+    def raise_column(at_axis, unit):
+        chunks = []
+        chips = lax.axis_size("seq")
+        dev_j = 0
+        while dev_j < chips:
+            chunks.append((dev_j, (dev_j + 1) % chips))
+            dev_j = dev_j + 1
+
+        def _put_clusters(y_new):
+            if len(y_new) == chips:
+                return y_new
+            local_next = lax.ppermute(y_new[0], "seq", chunks)
+            return _put_clusters([local_next, *y_new])
+
+        part_now = _put_clusters([unit])
+        fresh = jnp.concatenate(part_now, at_axis)
+        plain = lax.axis_index("seq")
+        return jnp.roll(fresh, (plain + 1) * unit.shape[at_axis], at_axis)
+
     local_rows = queries.shape[1]
     model_width = queries.shape[2]
     head_dim = model_width // HEADS
@@ -17,7 +37,7 @@
     peak_now = jnp.full((HEADS, local_rows), -jnp.inf, jnp.float32)
     totals = jnp.zeros((HEADS, local_rows), jnp.float32)
     accum = jnp.zeros((HEADS, local_rows, head_dim), jnp.float32)
-    key_block = lax.all_gather(keys, "seq", axis=1, tiled=True)
+    key_block = raise_column(1, keys)
     value_block = lax.all_gather(values, "seq", axis=1, tiled=True)
     count = key_block.shape[1]
     k_heads = key_block[0].reshape(count, HEADS, head_dim)

time: 372 us -> 353 us (0.949)
  waiting for transfers between devices: 172 us -> 151 us
    ppermute x0 -> x3, waiting for transfers between devices: none -> 52.6 us  [_put_clusters(): local_next = lax.ppermute(y_new[0], 'seq', chunks)]
    all_gather x1 -> x0, waiting for transfers between devices: 45.2 us -> none  [shards(): key_block = lax.all_gather(keys, 'seq', axis=1, tiled=True)]
    all_gather x1, waiting for transfers between devices: 39.7 us -> 11.8 us  [shards(): value_block = lax.all_gather(values, 'seq', axis=1, tiled=True)]
    unnamed x18 -> x25, local copies, waits for them, and re-layouts: 7.4 us -> 7.87 us
  transfers between devices with their start and end apart: 6 -> 8, of which waited for: 6 -> 8; matrix products, arithmetic and copies ran while one was open for 23% -> 24% of each run, Pallas kernels for 0% -> 0%
where the time goes in v1:
time: 353 us; the launch traced here: 352 us
  waiting for transfers between devices  151 us (43%)
  blocking collectives  69.2 us (20%)
  matrix products  55.3 us (16%)
  local copies, waits for them, and re-layouts  53.4 us (15%)
  between operations  14 us (4%)
  starting transfers between devices  7.88 us (2%)
    ppermute x3, waiting for transfers between devices, _put_clusters(): local_next = lax.ppermute(y_new[0], 'seq', chunks)  52.6 us
    all_to_all x1, blocking collectives, shards(): lax.all_to_all(send_x, ('seq', 'expert'), split_axis=0, concat_axis=0, ti...  34.6 us
    all_to_all x1, blocking collectives, shards(): lax.all_to_all(send_g, ('seq', 'expert'), split_axis=0, concat_axis=0, ti...  34.6 us
    reduce_scatter x1, waiting for transfers between devices, shards(): lax.psum_scatter(jnp.dot(hidden, w_second, preferred_element_type=jnp.flo...  32.5 us
    all_gather x1, waiting for transfers between devices, shards(): lax.all_gather(row_g, 'dp', axis=0, tiled=True)  25.8 us
    dot_general x1, matrix products, shards(): lax.dot_general(inputs, d_pre, (((0,), (0,)), ((), ())), preferred_elemen...  18.7 us
    all_gather x1, waiting for transfers between devices, shards(): lax.all_gather(row_x, 'dp', axis=0, tiled=True)  14.4 us
    all_to_all x1, waiting for transfers between devices, shards(): lax.all_to_all(summed.reshape(owners, capacity, model_width), ('seq', 'ex...  13.5 us
  transfers between devices with their start and end apart: 8, of which 8 were waited for; matrix products, arithmetic and copies ran while one was open for 24% of the time, Pallas kernels for 0%

profile of v1, /device:TPU:0, one launch (start us, length us, event | category | flops | bytes accessed | tf_op | source)
XLA Modules:
  0.0 352.3 jit_solution(2901848132763800016)
XLA Ops:
  7.2 1.4 copy.26
  8.6 3.1 collective-permute-start
  11.7 13.9 %collective-permute-done = bf16[1,128,2048]{1,2,0:T(8,128)(2,1)S(1)} collective-permute-done((bf16[1,128,2048]{1,2,0:T(8,128)(2,1)S(1)}, bf16[1,128,2048]{1,2,0:T(8,128)(2,1)S(1)}, u32[]{:S(2)}, u32[]{:S(2)}) %collective-permute-start) | collective-permute-done | bytes 524320 | tf_op jit(solution)/shard_map/ppermute | solution.py:24
  25.7 16.8 %collective-permute-done.1 = bf16[1,128,2048]{1,2,0:T(8,128)(2,1)S(1)} collective-permute-done((bf16[1,128,2048]{1,2,0:T(8,128)(2,1)S(1)}, bf16[1,128,2048]{1,2,0:T(8,128)(2,1)S(1)}, u32[]{:S(2)}, u32[]{:S(2)}) %collective-permute-start.1) | collective-permute-done | bytes 524320 | tf_op jit(solution)/shard_map/ppermute | solution.py:24
  42.5 0.7 fusion.43
  43.4 1.1 copy.41
  44.6 2.2 copy.34
  47.0 21.9 %collective-permute-done.2 = bf16[1,128,2048]{1,2,0:T(8,128)(2,1)S(1)} collective-permute-done((bf16[1,128,2048]{1,2,0:T(8,128)(2,1)S(1)}, bf16[1,128,2048]{1,2,0:T(8,128)(2,1)S(1)}, u32[]{:S(2)}, u32[]{:S(2)}) %collective-permute-start.2) | collective-permute-done | bytes 524320 | tf_op jit(solution)/shard_map/ppermute | solution.py:24
  69.0 0.2 constant_dynamic-update-slice_fusion.6
  69.2 0.2 constant_dynamic-update-slice_fusion.5
  69.4 0.2 constant_dynamic-update-slice_fusion.4
  69.6 0.2 constant_dynamic-update-slice_fusion.3
  69.8 0.2 constant_dynamic-update-slice_fusion.2
  70.0 0.2 constant_dynamic-update-slice_fusion.1
  70.1 0.2 constant_dynamic-update-slice_fusion
  70.3 0.2 constant_dynamic-slice_fusion
  70.6 0.9 bitcast_reduce_fusion
  71.6 2.0 copy-done.2
  73.5 0.7 fusion.15
  74.3 11.8 %all-gather.4.cloned.1.call-done = bf16[1,512,2048]{2,1,0:T(8,128)(2,1)} async-done(((bf16[1,128,2048]{2,1,0:T(8,128)(2,1)}), bf16[1,512,2048]{2,1,0:T(8,128)(2,1)}) %all-gather.4.cloned.1.call-update) | async-done | bytes 2097168 | tf_op jit(solution)/shard_map/all_gather | solution.py:41
  86.1 2.9 copy.31
  89.0 4.7 %multiply_reduce_fusion = (f32[128]{0:T(128)S(1)}, f32[128,16,128]{0,2,1:T(8,128)}) fusion(f32[128,16,128]{0,2,1:T(8,128)} %bitcast.77, f32[128,16]{0,1:T(8,128)S(1)} %bitcast_add_fusion.2, bf16[512,16,128]{0,2,1:T(8,128)(2,1)S(1)} %bitcast.75, f32[16,512,128]{2,1,0:T(8,128)} %copy-done.2, f32[16,128]{1,0:T(8,128)S(1)} %get-tuple-element.3, ...), kind=kOutput, calls=%fused_computation.35 | convolution fusion | flops 272891776 | bytes 8413696 | tf_op jit(solution)/shard_map/hst,thd->hsd/dot_general | solution.py:53
  93.7 1.6 copy.33
  95.3 1.5 convolution_convert_fusion.2
  96.8 1.4 reshape.62
  98.2 34.6 %all_to_all.15 = bf16[8,34,2048]{2,1,0:T(8,128)(2,1)S(1)} all-to-all(bf16[8,34,2048]{2,1,0:T(8,128)(2,1)S(1)} %reshape.62), channel_id=1, replica_groups=mesh['dp'=4,'seq'=4,'expert'=2] {'seq','expert'}, dimensions={0} | all-to-all | bytes 2228224 | tf_op jit(solution)/shard_map/all_to_all | solution.py:79
  132.8 1.6 copy.35
  134.5 1.4 convolution_convert_fusion.1
  136.0 1.4 reshape.66
  137.4 34.6 %all_to_all.16 = bf16[8,34,2048]{2,1,0:T(8,128)(2,1)S(1)} all-to-all(bf16[8,34,2048]{2,1,0:T(8,128)(2,1)S(1)} %reshape.66), channel_id=1, replica_groups=mesh['dp'=4,'seq'=4,'expert'=2] {'seq','expert'}, dimensions={0} | all-to-all | bytes 2228224 | tf_op jit(solution)/shard_map/all_to_all | solution.py:80
  172.0 1.6 copy.37
  173.7 14.4 %all-gather.6.cloned.1.call-done = bf16[32,34,2048]{2,0,1:T(8,128)(2,1)} async-done(((bf16[8,34,2048]{2,0,1:T(8,128)(2,1)}), bf16[32,34,2048]{2,0,1:T(8,128)(2,1)}) %all-gather.6.cloned.1.call-update) | async-done | bytes 4456464 | tf_op jit(solution)/shard_map/all_gather | solution.py:83
  188.1 7.1 %copy.36 = bf16[32,34,2048]{2,1,0:T(8,128)(2,1)} copy(bf16[32,34,2048]{2,0,1:T(8,128)(2,1)} %all-gather.6.cloned.1.call-done) | data formatting | bytes 8912896 | tf_op jit(solution)/shard_map/all_gather | solution.py:83
  195.2 7.4 %reshape.63 = bf16[1088,2048]{1,0:T(8,128)(2,1)} reshape(bf16[32,34,2048]{2,1,0:T(8,128)(2,1)} %copy.36) | data formatting | bytes 8912896 | tf_op jit(solution)/shard_map/reshape | solution.py:87
  202.6 8.0 %fusion.12 = f32[1088,1024]{1,0:T(8,128)S(1)} fusion(bf16[1088,2048]{1,0:T(8,128)(2,1)} %reshape.63, bf16[1,2048,1024]{2,1,0:T(8,128)(2,1)} %param.16), kind=kOutput, calls=%fused_computation.14 | convolution fusion | flops 4563402752 | bytes 13107200 | tf_op jit(solution)/shard_map/dot_general | solution.py:91
  210.6 2.1 copy-done.7
  212.7 6.7 %convolution_convert_fusion = bf16[1088,2048]{1,0:T(8,128)(2,1)} fusion(bf16[1,1024,2048]{2,1,0:T(8,128)(2,1)S(1)} %copy-done.6, f32[1088,1024]{1,0:T(8,128)S(1)} %fusion.12), kind=kOutput, calls=%fused_computation | convolution fusion | flops 4575657984 | bytes 13107200 | tf_op jit(solution)/shard_map/dot_general | solution.py:105
  219.5 25.8 %all-gather.8.cloned.1.call-done = bf16[32,34,2048]{2,0,1:T(8,128)(2,1)} async-done(((bf16[8,34,2048]{2,0,1:T(8,128)(2,1)}), bf16[32,34,2048]{2,0,1:T(8,128)(2,1)}) %all-gather.8.cloned.1.call-update) | async-done | bytes 4456464 | tf_op jit(solution)/shard_map/all_gather | solution.py:84
  245.3 7.1 %copy.38 = bf16[32,34,2048]{2,1,0:T(8,128)(2,1)} copy(bf16[32,34,2048]{2,0,1:T(8,128)(2,1)} %all-gather.8.cloned.1.call-done) | data formatting | bytes 8912896 | tf_op jit(solution)/shard_map/all_gather | solution.py:84
  252.4 7.4 %reshape.67 = bf16[1088,2048]{1,0:T(8,128)(2,1)} reshape(bf16[32,34,2048]{2,1,0:T(8,128)(2,1)} %copy.38) | data formatting | bytes 8912896 | tf_op jit(solution)/shard_map/reshape | solution.py:88
  259.8 10.7 %convert_bitcast_fusion = bf16[1,1024,2048]{2,1,0:T(8,128)(2,1)} fusion(bf16[1088,2048]{1,0:T(8,128)(2,1)} %reshape.67, f32[1088,1024]{1,0:T(8,128)} %copy-done.7), kind=kOutput, calls=%fused_computation.19 | convolution fusion | flops 4575526912 | bytes 13107200 | tf_op jit(solution)/shard_map/dot_general | solution.py:101
  270.5 32.5 %reduce-scatter.2.cloned.1.call-done = bf16[272,2048]{1,0:T(8,128)(2,1)} async-done(((bf16[1088,2048]{1,0:T(8,128)(2,1)}), bf16[272,2048]{1,0:T(8,128)(2,1)}) %reduce-scatter.2.cloned.1.call-update) | async-done | bytes 1114128 | tf_op jit(solution)/shard_map/reduce_scatter | solution.py:104
  303.0 2.3 reshape.64
  305.3 4.6 %all-to-all-start.1 = ((bf16[8,34,2048]{2,1,0:T(8,128)(2,1)}), bf16[8,34,2048]{2,1,0:T(8,128)(2,1)S(1)}, u32[]{:S(2)}, u32[]{:S(2)}) async-start(bf16[8,34,2048]{2,1,0:T(8,128)(2,1)} %reshape.64), calls=%async_computation.2 | async-start | bytes 2621440 | tf_op jit(solution)/shard_map/all_to_all | solution.py:110
  309.9 18.7 %convert_bitcast_fusion.1 = bf16[1,2048,1024]{2,1,0:T(8,128)(2,1)} fusion(bf16[1088,2048]{1,0:T(8,128)(2,1)} %reshape.63, f32[1088,1024]{1,0:T(8,128)} %copy-done.7, bf16[1088,2048]{1,0:T(8,128)(2,1)} %reshape.67, bf16[1,1024,2048]{2,1,0:T(8,128)(2,1)} %param.17), kind=kOutput, calls=%fused_computation.20 | convolution fusion | flops 9151184896 | bytes 21757952 | tf_op jit(solution)/shard_map/dot_general | solution.py:98
  328.6 13.5 %all-to-all-done.1 = bf16[8,34,2048]{2,1,0:T(8,128)(2,1)S(1)} async-done(((bf16[8,34,2048]{2,1,0:T(8,128)(2,1)}), bf16[8,34,2048]{2,1,0:T(8,128)(2,1)S(1)}, u32[]{:S(2)}, u32[]{:S(2)}) %all-to-all-start.1) | async-done | bytes 1114144 | tf_op jit(solution)/shard_map/all_to_all | solution.py:110
  342.1 1.2 reshape.65
  343.3 2.5 fusion.18
  (31 shorter events, 0.8 us)
Async XLA Ops:
  7.2 127.4 %copy-start = (bf16[1,128,2048]{2,1,0:T(8,128)(2,1)S(1)}, bf16[1,128,2048]{2,1,0:T(8,128)(2,1)}, u32[]{:S(2)}) copy-start(bf16[1,128,2048]{2,1,0:T(8,128)(2,1)} %param.13) | copy-start | bytes 1572868
  7.2 39.6 %copy-start.5 = (s32[1,128,1]{1,2,0:T(1,128)S(1)}, s32[1,128,1]{1,2,0:T(1,128)}, u32[]{:S(2)}) copy-start(s32[1,128,1]{1,2,0:T(1,128)} %param.14) | copy-start | bytes 1540
  7.2 78.9 %all-gather.4.cloned.1.call-start = ((), (), s32[]{:S(2)}) async-start(), calls=%async_computation.4 | async-start | bytes 2621440 | tf_op jit(solution)/shard_map/all_gather | solution.py:41
  8.6 17.1 %collective-permute-start = (bf16[1,128,2048]{1,2,0:T(8,128)(2,1)S(1)}, bf16[1,128,2048]{1,2,0:T(8,128)(2,1)S(1)}, u32[]{:S(2)}, u32[]{:S(2)}) collective-permute-start(bf16[1,128,2048]{1,2,0:T(8,128)(2,1)S(1)} %copy.26), channel_id=1, source_target_pairs={{0,2},{2,4},{4,6},{6,0},{1,3},{3,5},{5,7},{7,1},{8,10},{10,12},{12... | collective-permute-start | bytes 1572872 | tf_op jit(solution)/shard_map/ppermute | solution.py:24
  25.7 16.9 %collective-permute-start.1 = (bf16[1,128,2048]{1,2,0:T(8,128)(2,1)S(1)}, bf16[1,128,2048]{1,2,0:T(8,128)(2,1)S(1)}, u32[]{:S(2)}, u32[]{:S(2)}) collective-permute-start(bf16[1,128,2048]{1,2,0:T(8,128)(2,1)S(1)} %collective-permute-done), channel_id=1, source_target_pairs={{0,2},{2,4},{4,6},{6,0},{1,3},{3,5},{5,7},{7,1},{8,10},{10,12},{12... | collective-permute-start | bytes 1572872 | tf_op jit(solution)/shard_map/ppermute | solution.py:24
  25.7 162.4 %all-gather.6.cloned.1.call-start = ((), (), s32[]{:S(2)}) async-start(), calls=%async_computation.5 | async-start | bytes 5570560 | tf_op jit(solution)/shard_map/all_gather | solution.py:83
  42.5 26.4 %collective-permute-start.2 = (bf16[1,128,2048]{1,2,0:T(8,128)(2,1)S(1)}, bf16[1,128,2048]{1,2,0:T(8,128)(2,1)S(1)}, u32[]{:S(2)}, u32[]{:S(2)}) collective-permute-start(bf16[1,128,2048]{1,2,0:T(8,128)(2,1)S(1)} %collective-permute-done.1), channel_id=1, source_target_pairs={{0,2},{2,4},{4,6},{6,0},{1,3},{3,5},{5,7},{7,1},{8,10},{10,12},{12... | collective-permute-start | bytes 1572872 | tf_op jit(solution)/shard_map/ppermute | solution.py:24
  71.5 2.0 copy-start.2
  89.0 6.3 %copy-start.3 = (bf16[1,128,2048]{2,1,0:T(8,128)(2,1)S(1)}, bf16[1,128,2048]{2,1,0:T(8,128)(2,1)}, u32[]{:S(2)}) copy-start(bf16[1,128,2048]{2,1,0:T(8,128)(2,1)} %param.12) | copy-start | bytes 1572868
  89.0 6.3 %copy-start.4 = (f32[2048]{0:T(1024)S(1)}, f32[2048]{0:T(1024)}, u32[]{:S(2)}) copy-start(f32[2048]{0:T(1024)} %param.15) | copy-start | bytes 24580
  134.5 110.8 %all-gather.8.cloned.1.call-start = ((), (), s32[]{:S(2)}) async-start(), calls=%async_computation.7 | async-start | bytes 5570560 | tf_op jit(solution)/shard_map/all_gather | solution.py:84
  173.6 129.4 %reduce-scatter.2.cloned.1.call-start = ((), (), s32[]{:S(2)}) async-start(), calls=%async_computation.6 | async-start | bytes 5570560 | tf_op jit(solution)/shard_map/reduce_scatter | solution.py:104
  202.6 10.1 %copy-start.6 = (bf16[1,1024,2048]{2,1,0:T(8,128)(2,1)S(1)}, bf16[1,1024,2048]{2,1,0:T(8,128)(2,1)}, u32[]{:S(2)}) copy-start(bf16[1,1024,2048]{2,1,0:T(8,128)(2,1)} %param.17) | copy-start | bytes 12582916
  210.6 2.1 copy-start.7
  305.3 36.8 %all-to-all-start.1 = ((bf16[8,34,2048]{2,1,0:T(8,128)(2,1)}), bf16[8,34,2048]{2,1,0:T(8,128)(2,1)S(1)}, u32[]{:S(2)}, u32[]{:S(2)}) async-start(bf16[8,34,2048]{2,1,0:T(8,128)(2,1)} %reshape.64), calls=%async_computation.2 | async-start | bytes 2621440 | tf_op jit(solution)/shard_map/all_to_all | solution.py:110
  309.9 35.9 %copy-start.1 = (bf16[1,128,2048]{2,1,0:T(8,128)(2,1)S(1)}, bf16[1,128,2048]{2,1,0:T(8,128)(2,1)}, u32[]{:S(2)}) copy-start(bf16[1,128,2048]{2,1,0:T(8,128)(2,1)} %param.13) | copy-start | bytes 1572868
Sparse Core Ops, SparseCore 0:
  25.8 60.2 all-gather.3
  134.6 53.4 all-gather.5
  190.5 54.7 all-gather.7
  248.2 54.7 reduce-scatter.1
